TPU v7x, 512 devices: a whole 4x4x16 slice. The times are simulated.
512 devices in a mesh: grp: 16 (over z), tp: 32 (over y, x, core).
Axes of the slice: x: 4, y: 4, z: 16, core: 2. Of those that a mesh axis runs over, the one named last changes fastest.
Arguments:
- inputs: bfloat16 [61440, 8192], P('grp', 'tp'), may hold values from -6 to 6
- cotangent: bfloat16 [61440, 8192], P('grp', 'tp'), may hold values from -0.059814453 to 0.059814453
- factor_a: bfloat16 [64, 8192, 128], P('grp', 'tp'), may hold values from -0.0625 to 0.0625
- factor_b: bfloat16 [64, 128, 8192], P('grp', None, 'tp'), may hold values from -0.5 to 0.5
- adapter_slot: int32 [64], replicated, may hold values from 0 to 63, as said below
- seg_adapter: int32 [16, 30], replicated, may hold values from 0 to 63, as said below
Outputs:
- factor_a_grad: bfloat16 [64, 8192, 128], P('grp', 'tp')
- factor_b_grad: bfloat16 [64, 128, 8192], P('grp', None, 'tp')
Inputs may be any that keep to these rules, and one draw needn't show every extreme that they name: `adapter_slot`: A permutation: slot s lies on index s // 4 of grp. `seg_adapter`: within one micro-batch, all segments whose adapters' slots lie on the same index of grp use the same adapter.
All inputs are finite; a program needn't handle non-finite values.
Results may differ from a plain program's by a relative error of at most 0.0057.
Values may be sent and summed in bfloat16 or wider, within the bound.
A program may use at most 64 MiB of HBM per device.

v0:
```python
import jax
import jax.numpy as jnp
from jax import lax
from jax.sharding import PartitionSpec as P


def body(inputs, cotangent, factor_a, factor_b, adapter_slot, seg_adapter):
    groups = lax.axis_size("grp")
    owned_count = factor_a.shape[0]
    features = inputs.shape[1]
    rank_size = factor_a.shape[2]
    seg_count = seg_adapter.shape[1]
    seg_rows = inputs.shape[0] // seg_count
    total_adapters = adapter_slot.shape[0]
    my_group = lax.axis_index("grp")
    matches = seg_adapter[:, :, None] == jnp.arange(total_adapters, dtype=jnp.int32)[None, None, :]
    slot_all = jnp.sum(jnp.where(matches, adapter_slot[None, None, :], 0), axis=2)
    owner_all = slot_all // owned_count
    local_all = slot_all % owned_count
    my_slots = lax.dynamic_slice_in_dim(slot_all, my_group, 1, 0)[0]
    my_owners = lax.dynamic_slice_in_dim(owner_all, my_group, 1, 0)[0]
    is_mine = owner_all == my_group
    used_mask = jnp.any(
        is_mine[:, :, None]
        & (local_all[:, :, None] == jnp.arange(owned_count, dtype=jnp.int32)[None, None, :]),
        axis=1,
    )
    used_bf = used_mask.astype(jnp.bfloat16)
    tok_blocks = inputs.reshape(seg_count, seg_rows, features)
    cot_blocks = cotangent.reshape(seg_count, seg_rows, features)
    pieces = (
        lax.all_gather(factor_a, "grp", axis=0, tiled=True),
        lax.all_gather(factor_b, "grp", axis=0, tiled=True),
    )
    piece_rows = pieces[0].shape[0]
    picker = (my_slots[:, None] == jnp.arange(piece_rows, dtype=jnp.int32)[None, :]).astype(
        jnp.bfloat16
    )
    add_a = jnp.einsum("sn,npr->spr", picker, pieces[0], preferred_element_type=jnp.float32)
    add_b = jnp.einsum("sn,nrp->srp", picker, pieces[1], preferred_element_type=jnp.float32)
    seg_a = add_a.astype(jnp.bfloat16)
    seg_b = add_b.astype(jnp.bfloat16)
    part_input = jnp.einsum("stp,spr->str", tok_blocks, seg_a, preferred_element_type=jnp.float32)
    part_grad = jnp.einsum("stp,srp->str", cot_blocks, seg_b, preferred_element_type=jnp.float32)
    sum_input, sum_grad = lax.psum((part_input, part_grad), "tp")
    low_input = sum_input.astype(jnp.bfloat16)
    low_grad = sum_grad.astype(jnp.bfloat16)

    def add_segment(index, totals):
        owner = my_owners[index]
        tok_seg = lax.dynamic_index_in_dim(tok_blocks, index, 0, keepdims=False)
        cot_seg = lax.dynamic_index_in_dim(cot_blocks, index, 0, keepdims=False)
        grad_rows = lax.dynamic_index_in_dim(low_grad, index, 0, keepdims=False)
        input_rows = lax.dynamic_index_in_dim(low_input, index, 0, keepdims=False)
        delta_a = jnp.einsum("tp,tr->pr", tok_seg, grad_rows, preferred_element_type=jnp.float32)
        delta_b = jnp.einsum("tr,tp->rp", input_rows, cot_seg, preferred_element_type=jnp.float32)
        old_a = lax.dynamic_index_in_dim(totals[0], owner, 0, keepdims=False)
        old_b = lax.dynamic_index_in_dim(totals[1], owner, 0, keepdims=False)
        new_a = lax.dynamic_update_index_in_dim(totals[0], old_a + delta_a, owner, 0)
        new_b = lax.dynamic_update_index_in_dim(totals[1], old_b + delta_b, owner, 0)
        return (new_a, new_b)

    start = (
        jnp.zeros((groups, features, rank_size), jnp.float32),
        jnp.zeros((groups, rank_size, features), jnp.float32),
    )
    acc_a, acc_b = lax.fori_loop(0, seg_count, add_segment, start)
    group_a = acc_a.astype(jnp.bfloat16)
    group_b = acc_b.astype(jnp.bfloat16)
    back_a, back_b = (
        lax.all_to_all(group_a, "grp", split_axis=0, concat_axis=0, tiled=True),
        lax.all_to_all(group_b, "grp", split_axis=0, concat_axis=0, tiled=True),
    )
    grad_a = jnp.einsum("gj,gpr->jpr", used_bf, back_a, preferred_element_type=jnp.float32)
    grad_b = jnp.einsum("gj,grp->jrp", used_bf, back_b, preferred_element_type=jnp.float32)
    return (grad_a.astype(jnp.bfloat16), grad_b.astype(jnp.bfloat16))


def solution(mesh):
    return jax.shard_map(
        body,
        mesh=mesh,
        in_specs=(
            P("grp", "tp"),
            P("grp", "tp"),
            P("grp", "tp", None),
            P("grp", None, "tp"),
            P(),
            P(),
        ),
        out_specs=(P("grp", "tp", None), P("grp", None, "tp")),
        check_vma=False,
    )
```

profile of v0, /device:TPU:1, one launch (start us, length us, event | category | flops | bytes accessed | tf_op | source)
XLA Modules:
  0.0 626.5 jit_solution(16726001517277021135)
XLA Ops:
  9.4 1.3 select_reduce_fusion
  11.1 73.5 %all-gather.5.cloned.1.call-done = bf16[64,256,128]{2,1,0:T(8,128)(2,1)} async-done(((bf16[4,256,128]{2,1,0:T(8,128)(2,1)}), bf16[64,256,128]{2,1,0:T(8,128)(2,1)}) %all-gather.5.cloned.1.call-update) | async-done | bytes 4194320 | tf_op jit(solution)/shard_map/all_gather | solution.py:32
  84.6 5.3 fusion.25
  89.9 1.3 fusion.31
  91.3 69.9 %all-gather.3.cloned.1.call-done = bf16[64,128,256]{2,1,0:T(8,128)(2,1)} async-done(((bf16[4,128,256]{2,1,0:T(8,128)(2,1)}), bf16[64,128,256]{2,1,0:T(8,128)(2,1)}) %all-gather.3.cloned.1.call-update) | async-done | bytes 4194320 | tf_op jit(solution)/shard_map/all_gather | solution.py:33
  161.1 5.3 fusion.22
  166.5 2.6 fusion.28
  169.1 151.8 %all-reduce.2 = (bf16[30,128,128]{1,2,0:T(8,128)(2,1)S(1)}, bf16[30,128,128]{1,2,0:T(8,128)(2,1)}) all-reduce(f32[30,128,128]{1,2,0:T(8,128)} %fusion.28, f32[30,128,128]{1,2,0:T(8,128)S(1)} %fusion.31), channel_id=1, replica_groups=mesh['grp'=16,'tp'=32] {'tp'}, use_global_device_ids=true, to_apply=%region_2.3 | all-reduce | flops 983040 | bytes 5898240 | tf_op jit(solution)/shard_map/psum | solution.py:45
  321.2 1.5 broadcast_in_dim.43
  322.7 185.9 %while.15 = (s32[]{:T(128)}, f32[16,256,128]{2,1,0:T(8,128)}, f32[16,128,256]{2,1,0:T(8,128)S(1)}, s32[30]{0:T(128)S(1)}, bf16[30,128,256]{2,1,0:T(8,128)(2,1)},...) while((s32[]{:T(128)}, f32[16,256,128]{2,1,0:T(8,128)}, ...), condition=%wide.region_5.6_spmd, body=%wide.region_4.5_spmd.sunk | while | flops 16842756 | bytes 1248427 | solution.py:67
  326.2 1.7 fusion.59
  327.9 1.0 fusion.60
  332.4 1.7 fusion.59
  334.1 1.0 fusion.60
  338.6 1.7 fusion.59
  344.8 1.7 fusion.59
  346.5 1.0 fusion.60
  351.0 1.7 fusion.59
  352.7 1.0 fusion.60
  357.2 1.7 fusion.59
  363.3 1.7 fusion.59
  365.0 1.0 fusion.60
  369.5 1.7 fusion.59
  371.2 1.0 fusion.60
  375.7 1.7 fusion.59
  377.4 1.0 fusion.60
  381.9 1.7 fusion.59
  388.1 1.7 fusion.59
  394.3 1.7 fusion.59
  396.0 1.0 fusion.60
  400.5 1.7 fusion.59
  406.7 1.7 fusion.59
  408.4 1.0 fusion.60
  412.9 1.7 fusion.59
  414.6 1.0 fusion.60
  419.1 1.7 fusion.59
  425.3 1.7 fusion.59
  431.5 1.7 fusion.59
  433.2 1.0 fusion.60
  437.7 1.7 fusion.59
  443.9 1.7 fusion.59
  445.6 1.0 fusion.60
  450.1 1.7 fusion.59
  456.3 1.7 fusion.59
  458.0 1.0 fusion.60
  462.5 1.7 fusion.59
  464.2 1.0 fusion.60
  468.7 1.7 fusion.59
  470.4 1.0 fusion.60
  474.9 1.7 fusion.59
  476.6 1.0 fusion.60
  481.1 1.7 fusion.59
  487.3 1.7 fusion.59
  493.5 1.7 fusion.59
  499.7 1.7 fusion.59
  501.4 1.0 fusion.60
  505.9 1.7 fusion.59
  507.6 1.0 fusion.60
  508.6 1.1 convert_element_type.32
  509.8 7.3 %all-to-all-start.1 = ((bf16[16,128,256]{2,1,0:T(8,128)(2,1)}), bf16[16,128,256]{2,1,0:T(8,128)(2,1)S(1)}, u32[]{:S(2)}, u32[]{:S(2)}) async-start(bf16[16,128,256]{2,1,0:T(8,128)(2,1)} %convert_element_type.32), calls=%async_computation.1 | async-start | bytes 2097152 | tf_op jit(solution)/shard_map/all_to_all | solution.py:72
  517.0 1.2 convert_element_type.30
  518.2 45.2 %all-to-all-done.1 = bf16[16,128,256]{2,1,0:T(8,128)(2,1)S(1)} async-done(((bf16[16,128,256]{2,1,0:T(8,128)(2,1)}), bf16[16,128,256]{2,1,0:T(8,128)(2,1)S(1)}, u32[]{:S(2)}, u32[]{:S(2)}) %all-to-all-start.1) | async-done | bytes 1048608 | tf_op jit(solution)/shard_map/all_to_all | solution.py:72
  563.3 10.3 %all-to-all-start = ((bf16[16,256,128]{2,1,0:T(8,128)(2,1)}), bf16[16,256,128]{2,1,0:T(8,128)(2,1)S(1)}, u32[]{:S(2)}, u32[]{:S(2)}) async-start(bf16[16,256,128]{2,1,0:T(8,128)(2,1)} %convert_element_type.30), calls=%async_computation | async-start | bytes 2097152 | tf_op jit(solution)/shard_map/all_to_all | solution.py:71
  575.3 42.9 %all-to-all-done = bf16[16,256,128]{2,1,0:T(8,128)(2,1)S(1)} async-done(((bf16[16,256,128]{2,1,0:T(8,128)(2,1)}), bf16[16,256,128]{2,1,0:T(8,128)(2,1)S(1)}, u32[]{:S(2)}, u32[]{:S(2)}) %all-to-all-start) | async-done | bytes 1048608 | tf_op jit(solution)/shard_map/all_to_all | solution.py:71
  (124 shorter events, 63.4 us)
Async XLA Ops:
  7.2 77.5 %all-gather.5.cloned.1.call-start = ((), (), s32[]{:S(2)}) async-start(), calls=%async_computation.3 | async-start | bytes 4456448 | tf_op jit(solution)/shard_map/all_gather | solution.py:32
  7.9 153.2 %all-gather.3.cloned.1.call-start = ((), (), s32[]{:S(2)}) async-start(), calls=%async_computation.2 | async-start | bytes 4456448 | tf_op jit(solution)/shard_map/all_gather | solution.py:33
  84.6 5.3 copy-start.1
  161.1 5.3 copy-start.2
  509.8 7.3 %copy-start = (f32[16,256,128]{2,1,0:T(8,128)S(1)}, f32[16,256,128]{2,1,0:T(8,128)}, u32[]{:S(2)}) copy-start(f32[16,256,128]{2,1,0:T(8,128)} %get-tuple-element.142) | copy-start | bytes 6291460
  509.8 53.6 %all-to-all-start.1 = ((bf16[16,128,256]{2,1,0:T(8,128)(2,1)}), bf16[16,128,256]{2,1,0:T(8,128)(2,1)S(1)}, u32[]{:S(2)}, u32[]{:S(2)}) async-start(bf16[16,128,256]{2,1,0:T(8,128)(2,1)} %convert_element_type.32), calls=%async_computation.1 | async-start | bytes 2097152 | tf_op jit(solution)/shard_map/all_to_all | solution.py:72
  563.3 54.9 %all-to-all-start = ((bf16[16,256,128]{2,1,0:T(8,128)(2,1)}), bf16[16,256,128]{2,1,0:T(8,128)(2,1)S(1)}, u32[]{:S(2)}, u32[]{:S(2)}) async-start(bf16[16,256,128]{2,1,0:T(8,128)(2,1)} %convert_element_type.30), calls=%async_computation | async-start | bytes 2097152 | tf_op jit(solution)/shard_map/all_to_all | solution.py:71
Sparse Core Ops, SparseCore 0:
  10.0 74.5 all-gather.4
  86.7 74.4 all-gather.2
where the time goes:
time: 638 us; the launch traced here: 626 us
  waiting for transfers between devices  233 us (37%)
  blocking collectives  152 us (24%)
  matrix products  97 us (15%)
  loops' own time  59.2 us (9%)
  local copies, waits for them, and re-layouts  49.9 us (8%)
  starting transfers between devices  17.7 us (3%)
  between operations  14.1 us (2%)
    psum x1, blocking collectives, body(): sum_input, sum_grad = lax.psum((part_input, part_grad), 'tp')  152 us
    all_gather x1, waiting for transfers between devices, body(): lax.all_gather(factor_a, 'grp', axis=0, tiled=True)  73.5 us
    all_gather x1, waiting for transfers between devices, body(): lax.all_gather(factor_b, 'grp', axis=0, tiled=True)  69.9 us
    another operation x1, loops' own time, body(): acc_a, acc_b = lax.fori_loop(0, seg_count, add_segment, start)  59.2 us
    dot_general x30, matrix products, add_segment(): jnp.einsum('tp,tr->pr', tok_seg, grad_rows, preferred_element_type=jnp.fl...  50.9 us
    all_to_all x1, waiting for transfers between devices, body(): lax.all_to_all(group_b, 'grp', split_axis=0, concat_axis=0, tiled=True)  45.2 us
    all_to_all x1, waiting for transfers between devices, body(): lax.all_to_all(group_a, 'grp', split_axis=0, concat_axis=0, tiled=True)  42.9 us
    dot_general x30, matrix products, add_segment(): jnp.einsum('tr,tp->rp', input_rows, cot_seg, preferred_element_type=jnp.f...  30.1 us
  transfers between devices with their start and end apart: 4, of which 4 were waited for; matrix products, arithmetic and copies ran while one was open for 2% of the time, Pallas kernels for 0%

commit v1 on v0

v1 whole, which is shorter than its diff:
```python
import functools

import jax
import jax.numpy as jnp
from jax import lax
from jax.experimental import pallas as pl
from jax.experimental.pallas import tpu as pltpu
from jax.sharding import PartitionSpec as P

MESH = pl.DeviceIdType.MESH
N = 16
OWN = 4
F32 = jnp.float32
BF16 = jnp.bfloat16
SEL, REL, PREV, LAST = 0, 256, 288, 320


def kernel(
    segs, chips, per,
    tab, x_hbm, c_hbm, fa, fb,
    oa, ob,
    xv, cv,
    gda, gdb, gsa, gsb, ssa, ssb, wa, wb,
    part, other, pair, pieces, low,
    ta, tb, ga, gb,
    rra, rrb, rda, rdb, sda, sdb,
    local_sem, gd_s, gd_r, gs_s, gs_r, rr_s, rr_r, rd_s, rd_r,
    c1_s, c1_r, rs_s, rs_r, ag_s, ag_r, c2_s, c2_r,
):
    me = lax.axis_index("grp")
    tp = lax.axis_index("tp")
    chip = tp // 2
    core = tp % 2
    half = chips * per
    mine = core * half
    theirs = (1 - core) * half
    up = {"grp": lax.rem(me + 1, N), "tp": tp}
    down = {"grp": lax.rem(me + N - 1, N), "tp": tp}
    nbr = (up, down)
    sib = {"grp": me, "tp": chip * 2 + 1 - core}

    def chip_dev(step):
        return {"grp": me, "tp": lax.rem(chip + step, chips) * 2 + core}

    def rcopy(src, dst, ss, rs, dev):
        return pltpu.make_async_remote_copy(
            src_ref=src, dst_ref=dst, send_sem=ss, recv_sem=rs,
            device_id=dev, device_id_type=MESH,
        )

    fac, gd, gs, ss, w, tok = (fb, fa), (gdb, gda), (gsb, gsa), (ssb, ssa), (wb, wa), (cv, xv)
    tot, grp, rr, rd, sd, out = (ta, tb), (ga, gb), (rra, rrb), (rda, rdb), (sda, sdb), (oa, ob)
    sign = (1, -1)

    def at(offset):
        return lax.rem(me + offset + 2 * N, N)

    def sel(g, o):
        return tab[SEL + g * N + o]

    barrier = pltpu.get_barrier_semaphore()
    for dev in (up, down, sib):
        pl.semaphore_signal(barrier, inc=1, device_id=dev, device_id_type=MESH)
    if chips > 1:
        @pl.loop(1, chips)
        def _(p):
            pl.semaphore_signal(barrier, inc=1, device_id=chip_dev(p), device_id_type=MESH)
    pl.semaphore_wait(barrier, 3 + chips - 1)

    def gd_copy(m, d, t, j, src):
        return rcopy(src, gd[m].at[d, t, j], gd_s.at[m, d, t, j], gd_r.at[m, d, t, j], nbr[d])

    def gather_first(m, j):
        for d in (0, 1):
            gd_copy(m, d, 0, j, fac[m].at[j]).start()

    def gather_dense(m, i):
        t, j = i // OWN, i % OWN
        for d in (0, 1):
            gd_copy(m, d, t, j, gd[m].at[d, t, j]).wait_recv()
            gd_copy(m, d, t + 1, j, gd[m].at[d, t, j]).start()

    def gs_copy(m, d, h, q, src):
        if q == 3:
            return rcopy(src.at[d], gs[m].at[d, h, q, d], gs_s.at[m, d, h, q], gs_r.at[m, d, h, q], nbr[d])
        return rcopy(src, gs[m].at[d, h, q], gs_s.at[m, d, h, q], gs_r.at[m, d, h, q], nbr[d])

    def pick(ref4, s):
        a = jnp.where(s == 0, ref4[0], ref4[1])
        b = jnp.where(s == 2, ref4[2], ref4[3])
        return jnp.where(s < 2, a, b)

    def gather_select(m):
        for d in (0, 1):
            for j in range(OWN):
                gd_copy(m, d, 3, j, gd[m].at[d, 3, j]).wait_recv()
            o = at(-4 * sign[d])
            for q in (3, 2, 1, 0):
                s = sel(at((q + 1) * sign[d]), o)
                ss[m][d, q] = pick(gd[m].at[d, 3], s)
                gs_copy(m, d, 0, q, ss[m].at[d, q]).start()

    def gather_tail(m, filler):
        for h in range(3):
            for q in range(3, h, -1):
                for d in (0, 1):
                    gs_copy(m, d, h, q, gs[m].at[d, h, q]).wait_recv()
                    gs_copy(m, d, h + 1, q, gs[m].at[d, h, q]).start()
            filler(h)
        for h in range(4):
            for d in (0, 1):
                gs_copy(m, d, h, h, gs[m].at[d, h, h]).wait_recv()

    def build(m):
        w[m][0] = pick(fac[m], sel(me, me))
        for d in (0, 1):
            for t in range(1, 5):
                w[m][(-t * sign[d]) % N] = pick(gd[m].at[d, t - 1], sel(me, at(-t * sign[d])))
            for h in range(3):
                w[m][(-(5 + h) * sign[d]) % N] = gs[m][d, h, h]
            w[m][8, d] = gs[m][d, 3, 3, d]

    def project(m, k):
        rows = tok[m][k]
        rel = tab[REL + k]
        if m == 0:
            f = w[m][rel].reshape(128, rows.shape[1])
            v = lax.dot_general(rows, f, (((1,), (1,)), ((), ())), preferred_element_type=F32)
        else:
            f = w[m][rel].reshape(rows.shape[1], 128)
            v = lax.dot_general(rows, f, (((1,), (0,)), ((), ())), preferred_element_type=F32)
        part[m, k] = v.astype(BF16)

    def core1(m):
        return rcopy(part.at[m, pl.ds(theirs, half)], other.at[m], c1_s.at[m], c1_r.at[m], sib)

    def rs_copy(m, p):
        dest = lax.rem(chip + p, chips)
        return rcopy(pair.at[m, pl.ds(dest * per, per)], pieces.at[m, p], rs_s.at[m, p], rs_r.at[m, p], chip_dev(p))

    def ag_copy(m, p):
        spot = low.at[m, pl.ds(mine + chip * per, per)]
        return rcopy(spot, spot, ag_s.at[m, p], ag_r.at[m, p], chip_dev(p))

    def ag_wait(m, p):
        src = lax.rem(chip - p + chips, chips)
        spot = low.at[m, pl.ds(mine + src * per, per)]
        rcopy(spot, spot, ag_s.at[m, p], ag_r.at[m, p], chip_dev(p)).wait_recv()

    def core2(m, base):
        spot = low.at[m, pl.ds(base, half)]
        return rcopy(spot, spot, c2_s.at[m], c2_r.at[m], sib)

    def reduce_start(m):
        core1(m).wait_recv()

        @pl.loop(0, half)
        def _(h):
            pair[m, h] = (part[m, mine + h].astype(F32) + other[m, h].astype(F32)).astype(BF16)

        if chips > 1:
            @pl.loop(1, chips)
            def _(p):
                rs_copy(m, p).start()

    def reduce_mid(m):
        if chips > 1:
            @pl.loop(1, chips)
            def _(p):
                rs_copy(m, p).wait_recv()
        for l in range(per):
            acc = pair[m, chip * per + l].astype(F32)
            if chips > 1:
                acc = lax.fori_loop(1, chips, lambda p, a: a + pieces[m, p, l].astype(F32), acc)
            low[m, mine + chip * per + l] = acc.astype(BF16)
        if chips > 1:
            @pl.loop(1, chips)
            def _(p):
                ag_copy(m, p).start()

    def reduce_end(m):
        if chips > 1:
            @pl.loop(1, chips)
            def _(p):
                ag_wait(m, p)
        core2(m, mine).start()

    def outer(r, k):
        prev = tab[PREV + k]
        if r == 0:
            v = lax.dot_general(xv[k], low[0, k], (((0,), (0,)), ((), ())), preferred_element_type=F32)
        else:
            v = lax.dot_general(low[1, k], cv[k], (((0,), (0,)), ((), ())), preferred_element_type=F32)
        tot[r][k] = tot[r][prev] + v

    def groups(r):
        @pl.loop(0, segs)
        def _(k):
            outer(r, k)

        @pl.loop(0, N)
        def _(g):
            grp[r][g] = tot[r][tab[LAST + g]].astype(BF16).reshape(grp[r].shape[1:])

    def rr_copy(r, d, h, q, src):
        if q == 3:
            return rcopy(src.at[d], rr[r].at[d, h, q, d], rr_s.at[r, d, h, q], rr_r.at[r, d, h, q], nbr[d])
        return rcopy(src, rr[r].at[d, h, q], rr_s.at[r, d, h, q], rr_r.at[r, d, h, q], nbr[d])

    def ret_own(r):
        for q in (3, 2, 1, 0):
            for d in (0, 1):
                rr_copy(r, d, 3 - q, q, grp[r].at[((5 + q) * sign[d]) % N]).start()

    def ret_raw(r):
        for h in range(3):
            for q in range(3, 2 - h, -1):
                for d in (0, 1):
                    rr_copy(r, d, h, q, rr[r].at[d, h, q]).wait_recv()
                    rr_copy(r, d, h + 1, q, rr[r].at[d, h, q]).start()

    def rd_copy(r, d, u, s):
        return rcopy(sd[r].at[d, u, s], rd[r].at[d, u, s], rd_s.at[r, d, u, s], rd_r.at[r, d, u, s], nbr[d])

    def masked(flag, v):
        return jnp.where(flag, v, jnp.zeros_like(v))

    def ret_combine(r):
        for d in (0, 1):
            for q in (3, 2, 1, 0):
                rr_copy(r, d, 3, q, rr[r].at[d, 3, q]).wait_recv()
            o = at(4 * sign[d])
            for s in range(OWN):
                acc = masked(sel(me, o) == s, grp[r][(4 * sign[d]) % N].astype(F32))
                for q in (0, 1, 2):
                    acc = acc + masked(sel(at(-(q + 1) * sign[d]), o) == s, rr[r][d, 3, q].astype(F32))
                far = masked(sel(at(-4 * sign[d]), o) == s, rr[r][d, 3, 3, d].astype(F32))
                sd[r][d, 0, s, d] = (acc[d] + far).astype(BF16)
                sd[r][d, 0, s, 1 - d] = acc[1 - d].astype(BF16)
                rd_copy(r, d, 0, s).start()

    def ret_dense(r, i):
        u, s = i // OWN, i % OWN
        for d in (0, 1):
            rd_copy(r, d, u, s).wait_recv()
            offset = (3 - u) * sign[d]
            own = grp[r][lax.rem(offset + N, N)].astype(F32)
            v = rd[r][d, u, s].astype(F32) + masked(sel(me, at(offset)) == s, own)
            sd[r][d, u + 1, s] = v.astype(BF16)
            rd_copy(r, d, u + 1, s).start()

    def ret_final(r):
        for s in range(OWN):
            v = masked(sel(me, me) == s, grp[r][0].astype(F32))
            for d in (0, 1):
                rd_copy(r, d, 3, s).wait_recv()
                v = v + rd[r][d, 3, s].astype(F32)
            out[r][s] = v.astype(BF16)

    def loop(lo, hi, f):
        if hi > lo:
            pl.loop(lo, hi)(f)

    for j in range(OWN):
        gather_first(0, j)
    copies = (
        pltpu.make_async_copy(c_hbm, cv, local_sem.at[0]),
        pltpu.make_async_copy(x_hbm, xv, local_sem.at[1]),
    )
    for cp in copies:
        cp.start()
    for r in (0, 1):
        tot[r][segs] = jnp.zeros(tot[r].shape[1:], F32)
        for k in range(segs, 2 * half):
            part[r, k] = jnp.zeros((128, 128), BF16)

    loop(0, 12, lambda i: gather_dense(0, i))
    gather_select(0)
    gather_first(1, 0)
    gather_tail(0, lambda h: gather_first(1, h + 1))
    build(0)
    for cp in copies:
        cp.wait()

    chunk = -(-segs // 3)

    def mixed(i):
        gather_dense(1, i)
        for e in range(chunk):
            k = i * chunk + e
            project(0, jnp.minimum(k, segs - 1) if chunk * 3 != segs else k)

    loop(0, 3, mixed)
    core1(0).start()
    loop(3, 5, lambda i: gather_dense(1, i))
    reduce_start(0)
    loop(5, 10, lambda i: gather_dense(1, i))
    reduce_mid(0)
    loop(10, 12, lambda i: gather_dense(1, i))
    gather_select(1)
    reduce_end(0)
    gather_tail(1, lambda h: None)
    build(1)
    core2(0, theirs).wait_recv()
    groups(0)
    ret_own(0)
    loop(0, segs, lambda k: project(1, k))
    core1(1).start()
    ret_raw(0)
    reduce_start(1)
    ret_combine(0)
    loop(0, 6, lambda i: ret_dense(0, i))
    reduce_mid(1)
    loop(6, 10, lambda i: ret_dense(0, i))
    reduce_end(1)
    loop(10, 12, lambda i: ret_dense(0, i))
    core2(1, theirs).wait_recv()
    groups(1)
    ret_own(1)
    ret_final(0)
    ret_raw(1)
    ret_combine(1)
    loop(0, 12, lambda i: ret_dense(1, i))
    ret_final(1)

    for m in (0, 1):
        core1(m).wait_send()
        core2(m, mine).wait_send()
        if chips > 1:
            @pl.loop(1, chips)
            def _(p):
                rs_copy(m, p).wait_send()
                ag_copy(m, p).wait_send()

        @pl.loop(0, 16)
        def _(i):
            for d in (0, 1):
                gd_copy(m, d, i // OWN, i % OWN, gd[m].at[d, 0, 0]).wait_send()
                rd_copy(m, d, i // OWN, i % OWN).wait_send()

        for d in (0, 1):
            for h in range(4):
                for q in range(3, h - 1, -1):
                    gs_copy(m, d, h, q, gs[m].at[d, h, q]).wait_send()
                for q in range(3, 2 - h, -1):
                    rr_copy(m, d, h, q, rr[m].at[d, h, q]).wait_send()


def tables(adapter_slot, seg_adapter):
    segs = seg_adapter.shape[1]
    me = lax.axis_index("grp")
    ids = jnp.arange(adapter_slot.shape[0], dtype=jnp.int32)
    hit = seg_adapter[:, :, None] == ids[None, None, :]
    slot = jnp.sum(jnp.where(hit, adapter_slot[None, None, :], 0), axis=2)
    owner, place = slot // OWN, slot % OWN
    groups = jnp.arange(N, dtype=jnp.int32)
    sel = jnp.max(jnp.where(owner[:, :, None] == groups[None, None, :], place[:, :, None], 0), axis=1)
    mine = lax.dynamic_slice_in_dim(owner, me, 1, 0)[0]
    rel = lax.rem(mine - me + N, N)
    ks = jnp.arange(segs, dtype=jnp.int32)
    before = (rel[:, None] == rel[None, :]) & (ks[None, :] < ks[:, None])
    prev = jnp.max(jnp.where(before, ks[None, :], -1), axis=1)
    prev = jnp.where(prev < 0, segs, prev)
    last = jnp.max(jnp.where(rel[None, :] == groups[:, None], ks[None, :], -1), axis=1)
    last = jnp.where(last < 0, segs, last)
    pad = jnp.zeros((32 - segs,), jnp.int32)
    return jnp.concatenate([sel.reshape(-1), rel, pad, prev, pad, last])


def body(chips, inputs, cotangent, factor_a, factor_b, adapter_slot, seg_adapter):
    segs = seg_adapter.shape[1]
    rows = inputs.shape[0] // segs
    feat = inputs.shape[1]
    per = -(-segs // (2 * chips))
    half = chips * per
    tab = tables(adapter_slot, seg_adapter)
    a_unit, b_unit = (2, feat // 2, 128), (2, 64, feat)
    bf = lambda *shape: pltpu.VMEM(shape, BF16)
    fl = lambda *shape: pltpu.VMEM(shape, F32)
    dma = lambda *shape: pltpu.SemaphoreType.DMA(shape)
    vm = pl.BlockSpec(memory_space=pltpu.VMEM)
    scratch = [
        bf(segs, rows, feat), bf(segs, rows, feat),
        bf(2, 4, 4, *a_unit), bf(2, 4, 4, *b_unit),
        bf(2, 4, 4, *a_unit), bf(2, 4, 4, *b_unit),
        bf(2, 4, *a_unit), bf(2, 4, *b_unit),
        bf(N, *a_unit), bf(N, *b_unit),
        bf(2, 2 * half, rows, 128), bf(2, half, rows, 128), bf(2, half, rows, 128),
        bf(2, chips, per, rows, 128), bf(2, 2 * half, rows, 128),
        fl(segs + 1, feat, 128), fl(segs + 1, 128, feat),
        bf(N, *a_unit), bf(N, *b_unit),
        bf(2, 4, 4, *a_unit), bf(2, 4, 4, *b_unit),
        bf(2, 4, 4, *a_unit), bf(2, 4, 4, *b_unit),
        bf(2, 4, 4, *a_unit), bf(2, 4, 4, *b_unit),
        dma(2),
    ] + [dma(2, 2, 4, 4)] * 8 + [
        dma(2), dma(2), dma(2, chips), dma(2, chips), dma(2, chips), dma(2, chips), dma(2), dma(2),
    ]
    grad_a, grad_b = pl.pallas_call(
        functools.partial(kernel, segs, chips, per),
        out_shape=(
            jax.ShapeDtypeStruct((OWN,) + a_unit, BF16),
            jax.ShapeDtypeStruct((OWN,) + b_unit, BF16),
        ),
        in_specs=[
            pl.BlockSpec(memory_space=pltpu.SMEM),
            pl.BlockSpec(memory_space=pl.ANY),
            pl.BlockSpec(memory_space=pl.ANY),
            vm, vm,
        ],
        out_specs=(vm, vm),
        scratch_shapes=scratch,
        compiler_params=pltpu.CompilerParams(
            collective_id=0, has_side_effects=True, vmem_limit_bytes=60 << 20
        ),
        name="adapter_backward",
    )(
        tab,
        inputs.reshape(segs, rows, feat),
        cotangent.reshape(segs, rows, feat),
        factor_a.reshape((OWN,) + a_unit),
        factor_b.reshape((OWN,) + b_unit),
    )
    return grad_a.reshape(factor_a.shape), grad_b.reshape(factor_b.shape)


def solution(mesh):
    return jax.shard_map(
        functools.partial(body, mesh.shape["tp"] // 2),
        mesh=mesh,
        in_specs=(
            P("grp", "tp"),
            P("grp", "tp"),
            P("grp", "tp", None),
            P("grp", None, "tp"),
            P(),
            P(),
        ),
        out_specs=(P("grp", "tp", None), P("grp", None, "tp")),
        check_vma=False,
    )
```

time: 638 us -> 196 us (0.31); the launches traced: 626 us -> 195 us
  waiting for transfers between devices: 233 us -> 0 us
  Pallas kernels: 0 us -> 188 us
  blocking collectives: 152 us -> 0 us
  matrix products: 97 us -> 0 us
  loops' own time: 59.2 us -> 0 us
  local copies, waits for them, and re-layouts: 49.9 us -> 5.02 us
  starting transfers between devices: 17.7 us -> 0 us
  between operations: 14.1 us -> 0.69 us
    pallas_call x0 -> x1, Pallas kernels: none -> 188 us  [body(): pl.pallas_call(functools.partial(kernel, segs, chips, per), out_shape=(ja...]
    psum x1 -> x0, blocking collectives: 152 us -> none  [body(): sum_input, sum_grad = lax.psum((part_input, part_grad), 'tp')]
    all_gather x2 -> x0, waiting for transfers between devices: 143 us -> none  [the longest x1 73.5 us: body(): lax.all_gather(factor_a, 'grp', axis=0, tiled=True)]
    dot_general x66 -> x0, matrix products: 97 us -> none  [the longest x30 50.9 us: add_segment(): jnp.einsum('tp,tr->pr', tok_seg, grad_rows, preferred_element_type=jnp.fl...]
    all_to_all x2 -> x0, waiting for transfers between devices: 88.1 us -> none  [the longest x1 45.2 us: body(): lax.all_to_all(group_b, 'grp', split_axis=0, concat_axis=0, tiled=True)]
    another operation x1 -> x0, loops' own time: 59.2 us -> none  [body(): acc_a, acc_b = lax.fori_loop(0, seg_count, add_segment, start)]
    dynamic_slice x91 -> x0, local copies, waits for them, and re-layouts: 45.8 us -> none  [the longest x30 27.6 us: add_segment(): old_a = lax.dynamic_index_in_dim(totals[0], owner, 0, keepdims=False)]
    all_to_all x2 -> x0, starting transfers between devices: 17.6 us -> none  [the longest x1 10.3 us: body(): lax.all_to_all(group_a, 'grp', split_axis=0, concat_axis=0, tiled=True)]
  transfers between devices with their start and end apart: 4 -> 0, of which waited for: 4 -> 0; matrix products, arithmetic and copies ran while one was open for 2% -> 0% of each run, Pallas kernels for 0% -> 0%
where the time goes in v1:
time: 196 us; the launch traced here: 195 us
  Pallas kernels  188 us (96%)
  local copies, waits for them, and re-layouts  5.02 us (3%)
  other arithmetic  2.18 us (1%)
    pallas_call x1, Pallas kernels, body(): pl.pallas_call(functools.partial(kernel, segs, chips, per), out_shape=(ja...  188 us
    unnamed x3, local copies, waits for them, and re-layouts  4.12 us

profile of v1, /device:TPU:1, one launch (start us, length us, event | category | flops | bytes accessed | tf_op | source)
XLA Modules:
  0.0 195.4 jit_solution(15323163747338899801)
XLA Ops:
  0.6 0.8 copy.11
  1.4 1.3 select_reduce_fusion
  2.8 0.1 copy.13
  2.9 0.2 fusion.1
  3.0 0.1 copy.12
  3.1 0.3 select_reduce_fusion.1
  3.5 0.1 reshape.73
  3.6 0.2 select_reduce_fusion.3
  3.8 0.1 select_reduce_fusion.2
  3.9 0.7 concatenate.3.tab
  4.5 187.5 %adapter_backward.1 = (bf16[4,2,128,128]{3,2,1,0:T(8,128)(2,1)}, bf16[4,2,64,256]{3,2,1,0:T(8,128)(2,1)}) custom-call(s32[336]{0:T(512)} %concatenate.3.tab, bf16[30,128,256]{2,1,0:T(8,128)(2,1)} %bitcast.6, bf16[30,128,256]{2,1,0:T(8,128)(2,1)} %bitcast.7, bf16[4,2,128,128]{3,2,1,0:T(8,128)(2,1)} %bitcast.8, bf16[4,2,64,256]{3,2,1,0:T(8,128)(2,1)} %bitcast.9), custom_call_target="tpu_custom_call" | custom-call | tf_op jit(solution)/shard_map/adapter_backward/pallas_call | solution.py:399
  192.1 1.7 copy.16
  193.7 1.7 copy.17
  (5 shorter events, 0.0 us)

commit v2 on v1

--- a/solution.py
+++ b/solution.py
@@ -12,18 +12,19 @@
 OWN = 4
 F32 = jnp.float32
 BF16 = jnp.bfloat16
-SEL, REL, PREV, LAST = 0, 256, 288, 320
+REL, LAST = 16, 48
 
 
 def kernel(
     segs, chips, per,
-    tab, x_hbm, c_hbm, fa, fb,
+    aslot, seg, x_hbm, c_hbm, fa, fb,
     oa, ob,
     xv, cv,
     gda, gdb, gsa, gsb, ssa, ssb, wa, wb,
     part, other, pair, pieces, low,
     ta, tb, ga, gb,
     rra, rrb, rda, rdb, sda, sdb,
+    vtab, tab,
     local_sem, gd_s, gd_r, gs_s, gs_r, rr_s, rr_r, rd_s, rd_r,
     c1_s, c1_r, rs_s, rs_r, ag_s, ag_r, c2_s, c2_r,
 ):
@@ -56,7 +57,7 @@
         return lax.rem(me + offset + 2 * N, N)
 
     def sel(g, o):
-        return tab[SEL + g * N + o]
+        return tab[g, o]
 
     barrier = pltpu.get_barrier_semaphore()
     for dev in (up, down, sib):
@@ -67,8 +68,41 @@
             pl.semaphore_signal(barrier, inc=1, device_id=chip_dev(p), device_id_type=MESH)
     pl.semaphore_wait(barrier, 3 + chips - 1)
 
+    def build_tables():
+        ids = seg[...]
+        zero = jnp.zeros_like(ids)
+        slot = lax.fori_loop(0, aslot.shape[0], lambda n, a: jnp.where(ids == n, aslot[n], a), zero)
+        owner, place = lax.shift_right_logical(slot, 2), slot & 3
+
+        def iota(rows, cols, dim):
+            return lax.broadcasted_iota(jnp.int32, (rows, cols), dim)
+
+        lane = iota(N, 128, 1)
+        chosen = jnp.zeros((N, 128), jnp.int32)
+        for o in range(N):
+            best = jnp.max(jnp.where(owner == o, place, 0), axis=1, keepdims=True)
+            chosen = jnp.where(lane == o, best, chosen)
+        vtab[0:N] = chosen
+        row = jnp.sum(jnp.where(iota(N, segs, 0) == me, owner, 0), axis=0, keepdims=True)
+        row = (row - me + N) & (N - 1)
+        wide = jnp.broadcast_to(row, (32, segs))
+        down32, right32 = iota(32, segs, 0), iota(32, segs, 1)
+        col = jnp.sum(jnp.where(down32 == right32, wide, 0), axis=1, keepdims=True)
+        prev = jnp.max(jnp.where((wide == col) & (right32 < down32), right32, -1), axis=1, keepdims=True)
+        prev = jnp.where(prev < 0, segs, prev)
+        vtab[REL:REL + 32] = jnp.where(iota(32, 128, 1) == 0, col, prev)
+        last = jnp.max(jnp.where(wide[0:N] == iota(N, segs, 0), iota(N, segs, 1), -1), axis=1, keepdims=True)
+        last = jnp.where(last < 0, segs, last)
+        vtab[LAST:LAST + N] = jnp.broadcast_to(last, (N, 128))
+        move = pltpu.make_async_copy(vtab, tab, local_sem.at[2])
+        move.start()
+        return move
+
+    def spot(h, q):
+        return (0, 4, 7, 9)[h] + q - h
+
     def gd_copy(m, d, t, j, src):
-        return rcopy(src, gd[m].at[d, t, j], gd_s.at[m, d, t, j], gd_r.at[m, d, t, j], nbr[d])
+        return rcopy(src, gd[m].at[d, t, j], gd_s.at[m, d], gd_r.at[m, d, t, j], nbr[d])
 
     def gather_first(m, j):
         for d in (0, 1):
@@ -82,8 +116,8 @@
 
     def gs_copy(m, d, h, q, src):
         if q == 3:
-            return rcopy(src.at[d], gs[m].at[d, h, q, d], gs_s.at[m, d, h, q], gs_r.at[m, d, h, q], nbr[d])
-        return rcopy(src, gs[m].at[d, h, q], gs_s.at[m, d, h, q], gs_r.at[m, d, h, q], nbr[d])
+            return rcopy(src.at[d], gs[m].at[d, h, q, d], gs_s.at[m, d], gs_r.at[m, d, spot(h, q)], nbr[d])
+        return rcopy(src, gs[m].at[d, h, q], gs_s.at[m, d], gs_r.at[m, d, spot(h, q)], nbr[d])
 
     def pick(ref4, s):
         a = jnp.where(s == 0, ref4[0], ref4[1])
@@ -122,30 +156,25 @@
 
     def project(m, k):
         rows = tok[m][k]
-        rel = tab[REL + k]
+        rel = tab[REL + k, 0]
         if m == 0:
             f = w[m][rel].reshape(128, rows.shape[1])
             v = lax.dot_general(rows, f, (((1,), (1,)), ((), ())), preferred_element_type=F32)
         else:
             f = w[m][rel].reshape(rows.shape[1], 128)
             v = lax.dot_general(rows, f, (((1,), (0,)), ((), ())), preferred_element_type=F32)
-        part[m, k] = v.astype(BF16)
+        part[m, k] = v
 
     def core1(m):
         return rcopy(part.at[m, pl.ds(theirs, half)], other.at[m], c1_s.at[m], c1_r.at[m], sib)
 
     def rs_copy(m, p):
         dest = lax.rem(chip + p, chips)
-        return rcopy(pair.at[m, pl.ds(dest * per, per)], pieces.at[m, p], rs_s.at[m, p], rs_r.at[m, p], chip_dev(p))
+        return rcopy(pair.at[m, pl.ds(dest * per, per)], pieces.at[m, p], rs_s.at[m], rs_r.at[m], chip_dev(p))
 
     def ag_copy(m, p):
         spot = low.at[m, pl.ds(mine + chip * per, per)]
-        return rcopy(spot, spot, ag_s.at[m, p], ag_r.at[m, p], chip_dev(p))
-
-    def ag_wait(m, p):
-        src = lax.rem(chip - p + chips, chips)
-        spot = low.at[m, pl.ds(mine + src * per, per)]
-        rcopy(spot, spot, ag_s.at[m, p], ag_r.at[m, p], chip_dev(p)).wait_recv()
+        return rcopy(spot, spot, ag_s.at[m], ag_r.at[m], chip_dev(p))
 
     def core2(m, base):
         spot = low.at[m, pl.ds(base, half)]
@@ -156,18 +185,20 @@
 
         @pl.loop(0, half)
         def _(h):
-            pair[m, h] = (part[m, mine + h].astype(F32) + other[m, h].astype(F32)).astype(BF16)
+            pair[m, h] = (part[m, mine + h] + other[m, h]).astype(BF16)
 
         if chips > 1:
             @pl.loop(1, chips)
             def _(p):
                 rs_copy(m, p).start()
 
+    def pieces_of(m, ss, rs):
+        span = pieces.at[m, pl.ds(1, chips - 1)]
+        return rcopy(span, span, ss.at[m], rs.at[m], sib)
+
     def reduce_mid(m):
         if chips > 1:
-            @pl.loop(1, chips)
-            def _(p):
-                rs_copy(m, p).wait_recv()
+            pieces_of(m, rs_s, rs_r).wait_recv()
         for l in range(per):
             acc = pair[m, chip * per + l].astype(F32)
             if chips > 1:
@@ -180,47 +211,54 @@
 
     def reduce_end(m):
         if chips > 1:
-            @pl.loop(1, chips)
-            def _(p):
-                ag_wait(m, p)
+            pieces_of(m, ag_s, ag_r).wait_recv()
         core2(m, mine).start()
 
     def outer(r, k):
-        prev = tab[PREV + k]
         if r == 0:
-            v = lax.dot_general(xv[k], low[0, k], (((0,), (0,)), ((), ())), preferred_element_type=F32)
-        else:
-            v = lax.dot_general(low[1, k], cv[k], (((0,), (0,)), ((), ())), preferred_element_type=F32)
-        tot[r][k] = tot[r][prev] + v
+            return lax.dot_general(xv[k], low[0, k], (((0,), (0,)), ((), ())), preferred_element_type=F32)
+        return lax.dot_general(low[1, k], cv[k], (((0,), (0,)), ((), ())), preferred_element_type=F32)
+
+    third = segs // 3
+    step = 5 if third % 5 == 0 else 1
+
+    def outer_third(r, part_no):
+        @pl.loop(0, third // step)
+        def _(i):
+            ks = [part_no * third + i * step + e for e in range(step)]
+            vs = [outer(r, k) for k in ks]
+            for k, v in zip(ks, vs):
+                tot[r][k] = tot[r][tab[REL + k, 1]] + v
+
+    def project_third(m, part_no):
+        for e in range(third):
+            project(m, part_no * third + e)
 
     def groups(r):
-        @pl.loop(0, segs)
-        def _(k):
-            outer(r, k)
-
-        @pl.loop(0, N)
-        def _(g):
-            grp[r][g] = tot[r][tab[LAST + g]].astype(BF16).reshape(grp[r].shape[1:])
+        @pl.loop(0, N // 4)
+        def _(i):
+            for e in range(4):
+                g = i * 4 + e
+                grp[r][g] = tot[r][tab[LAST + g, 0]].astype(BF16).reshape(grp[r].shape[1:])
 
     def rr_copy(r, d, h, q, src):
         if q == 3:
-            return rcopy(src.at[d], rr[r].at[d, h, q, d], rr_s.at[r, d, h, q], rr_r.at[r, d, h, q], nbr[d])
-        return rcopy(src, rr[r].at[d, h, q], rr_s.at[r, d, h, q], rr_r.at[r, d, h, q], nbr[d])
+            return rcopy(src.at[d], rr[r].at[d, h, q, d], rr_s.at[r, d], rr_r.at[r, d, spot(3 - h, q)], nbr[d])
+        return rcopy(src, rr[r].at[d, h, q], rr_s.at[r, d], rr_r.at[r, d, spot(3 - h, q)], nbr[d])
 
     def ret_own(r):
         for q in (3, 2, 1, 0):
             for d in (0, 1):
                 rr_copy(r, d, 3 - q, q, grp[r].at[((5 + q) * sign[d]) % N]).start()
 
-    def ret_raw(r):
-        for h in range(3):
-            for q in range(3, 2 - h, -1):
-                for d in (0, 1):
-                    rr_copy(r, d, h, q, rr[r].at[d, h, q]).wait_recv()
-                    rr_copy(r, d, h + 1, q, rr[r].at[d, h, q]).start()
+    def ret_raw(r, h):
+        for q in range(3, 2 - h, -1):
+            for d in (0, 1):
+                rr_copy(r, d, h, q, rr[r].at[d, h, q]).wait_recv()
+                rr_copy(r, d, h + 1, q, rr[r].at[d, h, q]).start()
 
     def rd_copy(r, d, u, s):
-        return rcopy(sd[r].at[d, u, s], rd[r].at[d, u, s], rd_s.at[r, d, u, s], rd_r.at[r, d, u, s], nbr[d])
+        return rcopy(sd[r].at[d, u, s], rd[r].at[d, u, s], rd_s.at[r, d], rd_r.at[r, d, u, s], nbr[d])
 
     def masked(flag, v):
         return jnp.where(flag, v, jnp.zeros_like(v))
@@ -261,34 +299,32 @@
         if hi > lo:
             pl.loop(lo, hi)(f)
 
-    for j in range(OWN):
-        gather_first(0, j)
     copies = (
         pltpu.make_async_copy(c_hbm, cv, local_sem.at[0]),
         pltpu.make_async_copy(x_hbm, xv, local_sem.at[1]),
     )
+    for j in range(OWN):
+        gather_first(0, j)
     for cp in copies:
         cp.start()
+    move = build_tables()
+    loop(0, 4, lambda i: gather_dense(0, i))
     for r in (0, 1):
         tot[r][segs] = jnp.zeros(tot[r].shape[1:], F32)
         for k in range(segs, 2 * half):
-            part[r, k] = jnp.zeros((128, 128), BF16)
-
-    loop(0, 12, lambda i: gather_dense(0, i))
+            part[r, k] = jnp.zeros((128, 128), F32)
+    move.wait()
+    for cp in copies:
+        cp.wait()
+    loop(4, 12, lambda i: gather_dense(0, i))
     gather_select(0)
     gather_first(1, 0)
     gather_tail(0, lambda h: gather_first(1, h + 1))
     build(0)
-    for cp in copies:
-        cp.wait()
-
-    chunk = -(-segs // 3)
 
     def mixed(i):
         gather_dense(1, i)
-        for e in range(chunk):
-            k = i * chunk + e
-            project(0, jnp.minimum(k, segs - 1) if chunk * 3 != segs else k)
+        project_third(0, i)
 
     loop(0, 3, mixed)
     core1(0).start()
@@ -299,26 +335,41 @@
     loop(10, 12, lambda i: gather_dense(1, i))
     gather_select(1)
     reduce_end(0)
-    gather_tail(1, lambda h: None)
-    build(1)
-    core2(0, theirs).wait_recv()
+
+    def fill(h):
+        if h == 0:
+            core2(0, theirs).wait_recv()
+        outer_third(0, h)
+
+    gather_tail(1, fill)
     groups(0)
     ret_own(0)
-    loop(0, segs, lambda k: project(1, k))
+    build(1)
+    project_third(1, 0)
+    ret_raw(0, 0)
+    project_third(1, 1)
+    ret_raw(0, 1)
+    project_third(1, 2)
     core1(1).start()
-    ret_raw(0)
+    ret_raw(0, 2)
+    ret_combine(0)
+    loop(0, 1, lambda i: ret_dense(0, i))
     reduce_start(1)
-    ret_combine(0)
-    loop(0, 6, lambda i: ret_dense(0, i))
+    loop(1, 6, lambda i: ret_dense(0, i))
     reduce_mid(1)
     loop(6, 10, lambda i: ret_dense(0, i))
     reduce_end(1)
-    loop(10, 12, lambda i: ret_dense(0, i))
+    loop(10, 11, lambda i: ret_dense(0, i))
     core2(1, theirs).wait_recv()
+    outer_third(1, 0)
+    loop(11, 12, lambda i: ret_dense(0, i))
+    outer_third(1, 1)
+    outer_third(1, 2)
     groups(1)
     ret_own(1)
     ret_final(0)
-    ret_raw(1)
+    for h in range(3):
+        ret_raw(1, h)
     ret_combine(1)
     loop(0, 12, lambda i: ret_dense(1, i))
     ret_final(1)
@@ -327,44 +378,14 @@
         core1(m).wait_send()
         core2(m, mine).wait_send()
         if chips > 1:
-            @pl.loop(1, chips)
-            def _(p):
-                rs_copy(m, p).wait_send()
-                ag_copy(m, p).wait_send()
-
-        @pl.loop(0, 16)
-        def _(i):
-            for d in (0, 1):
-                gd_copy(m, d, i // OWN, i % OWN, gd[m].at[d, 0, 0]).wait_send()
-                rd_copy(m, d, i // OWN, i % OWN).wait_send()
-
-        for d in (0, 1):
-            for h in range(4):
-                for q in range(3, h - 1, -1):
-                    gs_copy(m, d, h, q, gs[m].at[d, h, q]).wait_send()
-                for q in range(3, 2 - h, -1):
-                    rr_copy(m, d, h, q, rr[m].at[d, h, q]).wait_send()
-
-
-def tables(adapter_slot, seg_adapter):
-    segs = seg_adapter.shape[1]
-    me = lax.axis_index("grp")
-    ids = jnp.arange(adapter_slot.shape[0], dtype=jnp.int32)
-    hit = seg_adapter[:, :, None] == ids[None, None, :]
-    slot = jnp.sum(jnp.where(hit, adapter_slot[None, None, :], 0), axis=2)
-    owner, place = slot // OWN, slot % OWN
-    groups = jnp.arange(N, dtype=jnp.int32)
-    sel = jnp.max(jnp.where(owner[:, :, None] == groups[None, None, :], place[:, :, None], 0), axis=1)
-    mine = lax.dynamic_slice_in_dim(owner, me, 1, 0)[0]
-    rel = lax.rem(mine - me + N, N)
-    ks = jnp.arange(segs, dtype=jnp.int32)
-    before = (rel[:, None] == rel[None, :]) & (ks[None, :] < ks[:, None])
-    prev = jnp.max(jnp.where(before, ks[None, :], -1), axis=1)
-    prev = jnp.where(prev < 0, segs, prev)
-    last = jnp.max(jnp.where(rel[None, :] == groups[:, None], ks[None, :], -1), axis=1)
-    last = jnp.where(last < 0, segs, last)
-    pad = jnp.zeros((32 - segs,), jnp.int32)
-    return jnp.concatenate([sel.reshape(-1), rel, pad, prev, pad, last])
+            pieces_of(m, rs_s, rs_r).wait_send()
+            pieces_of(m, ag_s, ag_r).wait_send()
+        for d in (0, 1):
+            for buf, sem in ((gd, gd_s), (rd, rd_s)):
+                rcopy(buf[m].at[d], buf[m].at[d], sem.at[m, d], sem.at[m, d], nbr[d]).wait_send()
+            for buf, sem in ((gs, gs_s), (rr, rr_s)):
+                span = buf[m].at[d, pl.ds(0, 2)]
+                rcopy(span, span, sem.at[m, d], sem.at[m, d], nbr[d]).wait_send()
 
 
 def body(chips, inputs, cotangent, factor_a, factor_b, adapter_slot, seg_adapter):
@@ -373,7 +394,6 @@
     feat = inputs.shape[1]
     per = -(-segs // (2 * chips))
     half = chips * per
-    tab = tables(adapter_slot, seg_adapter)
     a_unit, b_unit = (2, feat // 2, 128), (2, 64, feat)
     bf = lambda *shape: pltpu.VMEM(shape, BF16)
     fl = lambda *shape: pltpu.VMEM(shape, F32)
@@ -385,17 +405,18 @@
         bf(2, 4, 4, *a_unit), bf(2, 4, 4, *b_unit),
         bf(2, 4, *a_unit), bf(2, 4, *b_unit),
         bf(N, *a_unit), bf(N, *b_unit),
-        bf(2, 2 * half, rows, 128), bf(2, half, rows, 128), bf(2, half, rows, 128),
+        fl(2, 2 * half, rows, 128), fl(2, half, rows, 128), bf(2, half, rows, 128),
         bf(2, chips, per, rows, 128), bf(2, 2 * half, rows, 128),
         fl(segs + 1, feat, 128), fl(segs + 1, 128, feat),
         bf(N, *a_unit), bf(N, *b_unit),
         bf(2, 4, 4, *a_unit), bf(2, 4, 4, *b_unit),
         bf(2, 4, 4, *a_unit), bf(2, 4, 4, *b_unit),
         bf(2, 4, 4, *a_unit), bf(2, 4, 4, *b_unit),
-        dma(2),
-    ] + [dma(2, 2, 4, 4)] * 8 + [
-        dma(2), dma(2), dma(2, chips), dma(2, chips), dma(2, chips), dma(2, chips), dma(2), dma(2),
-    ]
+        pltpu.VMEM((64, 128), jnp.int32), pltpu.SMEM((64, 128), jnp.int32),
+        dma(3),
+        dma(2, 2), dma(2, 2, 4, 4), dma(2, 2), dma(2, 2, 10),
+        dma(2, 2), dma(2, 2, 10), dma(2, 2), dma(2, 2, 4, 4),
+    ] + [dma(2)] * 8
     grad_a, grad_b = pl.pallas_call(
         functools.partial(kernel, segs, chips, per),
         out_shape=(
@@ -404,6 +425,7 @@
         ),
         in_specs=[
             pl.BlockSpec(memory_space=pltpu.SMEM),
+            vm,
             pl.BlockSpec(memory_space=pl.ANY),
             pl.BlockSpec(memory_space=pl.ANY),
             vm, vm,
@@ -415,7 +437,8 @@
         ),
         name="adapter_backward",
     )(
-        tab,
+        adapter_slot,
+        seg_adapter,
         inputs.reshape(segs, rows, feat),
         cotangent.reshape(segs, rows, feat),
         factor_a.reshape((OWN,) + a_unit),

time: 196 us -> 178 us (0.908)
  Pallas kernels: 188 us -> 174 us
  other arithmetic: 2.18 us -> 0 us
    pallas_call x1, Pallas kernels: 188 us -> 174 us  [body(): pl.pallas_call(functools.partial(kernel, segs, chips, per), out_shape=(ja...]
    unnamed x3 -> x2, local copies, waits for them, and re-layouts: 4.12 us -> 3.34 us
where the time goes in v2:
time: 178 us
  Pallas kernels  174 us (98%)
  local copies, waits for them, and re-layouts  3.34 us (2%)
    pallas_call x1, Pallas kernels, body(): pl.pallas_call(functools.partial(kernel, segs, chips, per), out_shape=(ja...  174 us

profile of v2, /device:TPU:1, one launch (start us, length us, event | category | flops | bytes accessed | tf_op | source)
XLA Modules:
  0.0 178.0 jit_solution(1775126864828886114)
XLA Ops:
  0.6 174.0 %adapter_backward.1 = (bf16[4,2,128,128]{3,2,1,0:T(8,128)(2,1)}, bf16[4,2,64,256]{3,2,1,0:T(8,128)(2,1)}) custom-call(s32[64]{0:T(128)} %aslot.1, s32[16,30]{1,0:T(8,128)} %seg.1, bf16[30,128,256]{2,1,0:T(8,128)(2,1)} %bitcast.6, bf16[30,128,256]{2,1,0:T(8,128)(2,1)} %bitcast.7, bf16[4,2,128,128]{3,2,1,0:T(8,128)(2,1)} %bitcast.8, ...), custom_call_target="tpu_custom_call" | custom-call | tf_op jit(solution)/shard_map/adapter_backward/pallas_call | solution.py:420
  174.7 1.7 copy.10
  176.3 1.7 copy.11

commit v3 on v2

--- a/solution.py
+++ b/solution.py
@@ -1,4 +1,5 @@
 import functools
+import math
 
 import jax
 import jax.numpy as jnp
@@ -40,8 +41,19 @@
     nbr = (up, down)
     sib = {"grp": me, "tp": chip * 2 + 1 - core}
 
+    side = math.isqrt(chips)
+
+    def hops(step):
+        return sum(min(e, side - e) for e in divmod(step, side))
+
+    others = sorted(range(1, chips), key=lambda step: -hops(step))
+
+    def chip_at(step):
+        dy, dx = divmod(step, side)
+        return lax.rem(chip // side + dy, side) * side + lax.rem(chip % side + dx, side)
+
     def chip_dev(step):
-        return {"grp": me, "tp": lax.rem(chip + step, chips) * 2 + core}
+        return {"grp": me, "tp": chip_at(step) * 2 + core}
 
     def rcopy(src, dst, ss, rs, dev):
         return pltpu.make_async_remote_copy(
@@ -62,10 +74,8 @@
     barrier = pltpu.get_barrier_semaphore()
     for dev in (up, down, sib):
         pl.semaphore_signal(barrier, inc=1, device_id=dev, device_id_type=MESH)
-    if chips > 1:
-        @pl.loop(1, chips)
-        def _(p):
-            pl.semaphore_signal(barrier, inc=1, device_id=chip_dev(p), device_id_type=MESH)
+    for p in others:
+        pl.semaphore_signal(barrier, inc=1, device_id=chip_dev(p), device_id_type=MESH)
     pl.semaphore_wait(barrier, 3 + chips - 1)
 
     def build_tables():
@@ -88,11 +98,23 @@
         wide = jnp.broadcast_to(row, (32, segs))
         down32, right32 = iota(32, segs, 0), iota(32, segs, 1)
         col = jnp.sum(jnp.where(down32 == right32, wide, 0), axis=1, keepdims=True)
-        prev = jnp.max(jnp.where((wide == col) & (right32 < down32), right32, -1), axis=1, keepdims=True)
-        prev = jnp.where(prev < 0, segs, prev)
+        size = 2 * half
+
+        def turn(k):
+            return jnp.where(k >= mine, k - mine, k - mine + size)
+
+        def back(best):
+            k = best + mine
+            return jnp.where(best < 0, size, jnp.where(k >= size, k - size, k))
+
+        right_turn, down_turn = turn(right32), turn(down32)
+        prev = back(jnp.max(
+            jnp.where((wide == col) & (right_turn < down_turn), right_turn, -1), axis=1, keepdims=True
+        ))
         vtab[REL:REL + 32] = jnp.where(iota(32, 128, 1) == 0, col, prev)
-        last = jnp.max(jnp.where(wide[0:N] == iota(N, segs, 0), iota(N, segs, 1), -1), axis=1, keepdims=True)
-        last = jnp.where(last < 0, segs, last)
+        last = back(jnp.max(
+            jnp.where(wide[0:N] == iota(N, segs, 0), right_turn[0:N], -1), axis=1, keepdims=True
+        ))
         vtab[LAST:LAST + N] = jnp.broadcast_to(last, (N, 128))
         move = pltpu.make_async_copy(vtab, tab, local_sem.at[2])
         move.start()
@@ -155,7 +177,7 @@
             w[m][8, d] = gs[m][d, 3, 3, d]
 
     def project(m, k):
-        rows = tok[m][k]
+        rows = tok[m][jnp.minimum(k, segs - 1)]
         rel = tab[REL + k, 0]
         if m == 0:
             f = w[m][rel].reshape(128, rows.shape[1])
@@ -169,7 +191,7 @@
         return rcopy(part.at[m, pl.ds(theirs, half)], other.at[m], c1_s.at[m], c1_r.at[m], sib)
 
     def rs_copy(m, p):
-        dest = lax.rem(chip + p, chips)
+        dest = chip_at(p)
         return rcopy(pair.at[m, pl.ds(dest * per, per)], pieces.at[m, p], rs_s.at[m], rs_r.at[m], chip_dev(p))
 
     def ag_copy(m, p):
@@ -187,10 +209,8 @@
         def _(h):
             pair[m, h] = (part[m, mine + h] + other[m, h]).astype(BF16)
 
-        if chips > 1:
-            @pl.loop(1, chips)
-            def _(p):
-                rs_copy(m, p).start()
+        for p in others:
+            rs_copy(m, p).start()
 
     def pieces_of(m, ss, rs):
         span = pieces.at[m, pl.ds(1, chips - 1)]
@@ -204,10 +224,8 @@
             if chips > 1:
                 acc = lax.fori_loop(1, chips, lambda p, a: a + pieces[m, p, l].astype(F32), acc)
             low[m, mine + chip * per + l] = acc.astype(BF16)
-        if chips > 1:
-            @pl.loop(1, chips)
-            def _(p):
-                ag_copy(m, p).start()
+        for p in others:
+            ag_copy(m, p).start()
 
     def reduce_end(m):
         if chips > 1:
@@ -216,23 +234,29 @@
 
     def outer(r, k):
         if r == 0:
-            return lax.dot_general(xv[k], low[0, k], (((0,), (0,)), ((), ())), preferred_element_type=F32)
-        return lax.dot_general(low[1, k], cv[k], (((0,), (0,)), ((), ())), preferred_element_type=F32)
-
-    third = segs // 3
-    step = 5 if third % 5 == 0 else 1
-
-    def outer_third(r, part_no):
-        @pl.loop(0, third // step)
+            return lax.dot_general(xv[jnp.minimum(k, segs - 1)], low[0, k], (((0,), (0,)), ((), ())), preferred_element_type=F32)
+        return lax.dot_general(low[1, k], cv[jnp.minimum(k, segs - 1)], (((0,), (0,)), ((), ())), preferred_element_type=F32)
+
+    quarter = -(-half // 2)
+    step = 4 if half % 8 == 0 else 1
+
+    def spans(base, part_no):
+        return base + part_no * quarter, min(quarter, half - part_no * quarter)
+
+    def outer_part(r, base, part_no):
+        lo, count = spans(base, part_no)
+
+        @pl.loop(0, count // step)
         def _(i):
-            ks = [part_no * third + i * step + e for e in range(step)]
+            ks = [lo + i * step + e for e in range(step)]
             vs = [outer(r, k) for k in ks]
             for k, v in zip(ks, vs):
                 tot[r][k] = tot[r][tab[REL + k, 1]] + v
 
-    def project_third(m, part_no):
-        for e in range(third):
-            project(m, part_no * third + e)
+    def project_part(m, base, part_no):
+        lo, count = spans(base, part_no)
+        for e in range(count):
+            project(m, lo + e)
 
     def groups(r):
         @pl.loop(0, N // 4)
@@ -246,16 +270,21 @@
             return rcopy(src.at[d], rr[r].at[d, h, q, d], rr_s.at[r, d], rr_r.at[r, d, spot(3 - h, q)], nbr[d])
         return rcopy(src, rr[r].at[d, h, q], rr_s.at[r, d], rr_r.at[r, d, spot(3 - h, q)], nbr[d])
 
+    def ret_send(r, q):
+        for d in (0, 1):
+            rr_copy(r, d, 3 - q, q, grp[r].at[((5 + q) * sign[d]) % N]).start()
+
     def ret_own(r):
-        for q in (3, 2, 1, 0):
-            for d in (0, 1):
-                rr_copy(r, d, 3 - q, q, grp[r].at[((5 + q) * sign[d]) % N]).start()
-
-    def ret_raw(r, h):
-        for q in range(3, 2 - h, -1):
+        for q in (3, 2, 1):
+            ret_send(r, q)
+
+    def ret_raw(r, part_no):
+        for h, q in (((0, 3), (1, 2), (2, 1)), ((1, 3), (2, 2)), ((2, 3),))[part_no]:
             for d in (0, 1):
                 rr_copy(r, d, h, q, rr[r].at[d, h, q]).wait_recv()
                 rr_copy(r, d, h + 1, q, rr[r].at[d, h, q]).start()
+        if part_no == 1:
+            ret_send(r, 0)
 
     def rd_copy(r, d, u, s):
         return rcopy(sd[r].at[d, u, s], rd[r].at[d, u, s], rd_s.at[r, d], rd_r.at[r, d, u, s], nbr[d])
@@ -310,9 +339,7 @@
     move = build_tables()
     loop(0, 4, lambda i: gather_dense(0, i))
     for r in (0, 1):
-        tot[r][segs] = jnp.zeros(tot[r].shape[1:], F32)
-        for k in range(segs, 2 * half):
-            part[r, k] = jnp.zeros((128, 128), F32)
+        tot[r][2 * half] = jnp.zeros(tot[r].shape[1:], F32)
     move.wait()
     for cp in copies:
         cp.wait()
@@ -321,14 +348,16 @@
     gather_first(1, 0)
     gather_tail(0, lambda h: gather_first(1, h + 1))
     build(0)
-
-    def mixed(i):
-        gather_dense(1, i)
-        project_third(0, i)
-
-    loop(0, 3, mixed)
+    gather_dense(1, 0)
+    project_part(0, theirs, 0)
+    gather_dense(1, 1)
+    project_part(0, theirs, 1)
     core1(0).start()
-    loop(3, 5, lambda i: gather_dense(1, i))
+    gather_dense(1, 2)
+    project_part(0, mine, 0)
+    gather_dense(1, 3)
+    project_part(0, mine, 1)
+    gather_dense(1, 4)
     reduce_start(0)
     loop(5, 10, lambda i: gather_dense(1, i))
     reduce_mid(0)
@@ -338,39 +367,44 @@
 
     def fill(h):
         if h == 0:
+            outer_part(0, mine, 0)
+            outer_part(0, mine, 1)
             core2(0, theirs).wait_recv()
-        outer_third(0, h)
+        else:
+            outer_part(0, theirs, h - 1)
 
     gather_tail(1, fill)
     groups(0)
     ret_own(0)
     build(1)
-    project_third(1, 0)
+    project_part(1, theirs, 0)
+    project_part(1, theirs, 1)
+    core1(1).start()
+    project_part(1, mine, 0)
+    project_part(1, mine, 1)
     ret_raw(0, 0)
-    project_third(1, 1)
     ret_raw(0, 1)
-    project_third(1, 2)
-    core1(1).start()
+    reduce_start(1)
     ret_raw(0, 2)
     ret_combine(0)
-    loop(0, 1, lambda i: ret_dense(0, i))
-    reduce_start(1)
-    loop(1, 6, lambda i: ret_dense(0, i))
+    loop(0, 3, lambda i: ret_dense(0, i))
     reduce_mid(1)
-    loop(6, 10, lambda i: ret_dense(0, i))
+    loop(3, 8, lambda i: ret_dense(0, i))
     reduce_end(1)
+    outer_part(1, mine, 0)
+    outer_part(1, mine, 1)
+    loop(8, 10, lambda i: ret_dense(0, i))
+    core2(1, theirs).wait_recv()
+    outer_part(1, theirs, 0)
     loop(10, 11, lambda i: ret_dense(0, i))
-    core2(1, theirs).wait_recv()
-    outer_third(1, 0)
+    outer_part(1, theirs, 1)
     loop(11, 12, lambda i: ret_dense(0, i))
-    outer_third(1, 1)
-    outer_third(1, 2)
     groups(1)
     ret_own(1)
-    ret_final(0)
     for h in range(3):
         ret_raw(1, h)
     ret_combine(1)
+    ret_final(0)
     loop(0, 12, lambda i: ret_dense(1, i))
     ret_final(1)
 
@@ -386,6 +420,11 @@
             for buf, sem in ((gs, gs_s), (rr, rr_s)):
                 span = buf[m].at[d, pl.ds(0, 2)]
                 rcopy(span, span, sem.at[m, d], sem.at[m, d], nbr[d]).wait_send()
+
+
+def finish(a_ref, b_ref, oa_ref, ob_ref):
+    oa_ref[...] = a_ref[...]
+    ob_ref[...] = b_ref[...]
 
 
 def body(chips, inputs, cotangent, factor_a, factor_b, adapter_slot, seg_adapter):
@@ -407,7 +446,7 @@
         bf(N, *a_unit), bf(N, *b_unit),
         fl(2, 2 * half, rows, 128), fl(2, half, rows, 128), bf(2, half, rows, 128),
         bf(2, chips, per, rows, 128), bf(2, 2 * half, rows, 128),
-        fl(segs + 1, feat, 128), fl(segs + 1, 128, feat),
+        fl(2 * half + 1, feat, 128), fl(2 * half + 1, 128, feat),
         bf(N, *a_unit), bf(N, *b_unit),
         bf(2, 4, 4, *a_unit), bf(2, 4, 4, *b_unit),
         bf(2, 4, 4, *a_unit), bf(2, 4, 4, *b_unit),
@@ -444,6 +483,13 @@
         factor_a.reshape((OWN,) + a_unit),
         factor_b.reshape((OWN,) + b_unit),
     )
+    grad_a, grad_b = pl.pallas_call(
+        finish,
+        out_shape=(jax.ShapeDtypeStruct(grad_a.shape, BF16), jax.ShapeDtypeStruct(grad_b.shape, BF16)),
+        in_specs=[vm, vm],
+        out_specs=(vm, vm),
+        name="finish",
+    )(grad_a, grad_b)
     return grad_a.reshape(factor_a.shape), grad_b.reshape(factor_b.shape)
 
 

time: 178 us -> 168 us (0.944)
  Pallas kernels: 174 us -> 167 us
  local copies, waits for them, and re-layouts: 3.34 us -> 0 us
    pallas_call x1, Pallas kernels: 174 us -> 165 us  [body(): pl.pallas_call(functools.partial(kernel, segs, chips, per), out_shape=(ja...]
    unnamed x2 -> x0, local copies, waits for them, and re-layouts: 3.34 us -> none
    pallas_call x0 -> x1, Pallas kernels: none -> 1.84 us  [body(): pl.pallas_call(finish, out_shape=(jax.ShapeDtypeStruct(grad_a.shape, BF16...]
where the time goes in v3:
time: 168 us; the launch traced here: 167 us
  Pallas kernels  167 us (99%)
    pallas_call x1, Pallas kernels, body(): pl.pallas_call(functools.partial(kernel, segs, chips, per), out_shape=(ja...  165 us

profile of v3, /device:TPU:1, one launch (start us, length us, event | category | flops | bytes accessed | tf_op | source)
XLA Modules:
  0.0 167.4 jit_solution(16093881460655651618)
XLA Ops:
  0.6 164.9 %adapter_backward.1 = (bf16[4,2,128,128]{3,2,1,0:T(8,128)(2,1)}, bf16[4,2,64,256]{3,2,1,0:T(8,128)(2,1)}) custom-call(s32[64]{0:T(128)} %aslot.1, s32[16,30]{1,0:T(8,128)} %seg.1, bf16[30,128,256]{2,1,0:T(8,128)(2,1)} %bitcast.6, bf16[30,128,256]{2,1,0:T(8,128)(2,1)} %bitcast.7, bf16[4,2,128,128]{3,2,1,0:T(8,128)(2,1)} %bitcast.8, ...), custom_call_target="tpu_custom_call" | custom-call | tf_op jit(solution)/shard_map/adapter_backward/pallas_call | solution.py:459
  165.6 1.8 %finish.1 = (bf16[4,2,128,128]{3,2,1,0:T(8,128)(2,1)}, bf16[4,2,64,256]{3,2,1,0:T(8,128)(2,1)}) custom-call(bf16[4,2,128,128]{3,2,1,0:T(8,128)(2,1)} %get-tuple-element.6.a_ref, bf16[4,2,64,256]{3,2,1,0:T(8,128)(2,1)} %get-tuple-element.7.b_ref), custom_call_target="tpu_custom_call" | custom-call | tf_op jit(solution)/shard_map/finish/pallas_call | solution.py:486

commit v4 on v3

--- a/solution.py
+++ b/solution.py
@@ -18,9 +18,9 @@
 
 def kernel(
     segs, chips, per,
-    aslot, seg, x_hbm, c_hbm, fa, fb,
+    slot_hbm, seg_hbm, x_hbm, c_hbm, a_hbm, b_hbm,
     oa, ob,
-    xv, cv,
+    xv, cv, fa, fb, aslot, seg,
     gda, gdb, gsa, gsb, ssa, ssb, wa, wb,
     part, other, pair, pieces, low,
     ta, tb, ga, gb,
@@ -76,6 +76,14 @@
         pl.semaphore_signal(barrier, inc=1, device_id=dev, device_id_type=MESH)
     for p in others:
         pl.semaphore_signal(barrier, inc=1, device_id=chip_dev(p), device_id_type=MESH)
+    copies = [
+        pltpu.make_async_copy(src, dst, local_sem.at[i])
+        for i, (src, dst) in enumerate((
+            (slot_hbm, aslot), (seg_hbm, seg), (b_hbm, fb), (a_hbm, fa), (c_hbm, cv), (x_hbm, xv),
+        ))
+    ]
+    for cp in copies:
+        cp.start()
     pl.semaphore_wait(barrier, 3 + chips - 1)
 
     def build_tables():
@@ -116,7 +124,7 @@
             jnp.where(wide[0:N] == iota(N, segs, 0), right_turn[0:N], -1), axis=1, keepdims=True
         ))
         vtab[LAST:LAST + N] = jnp.broadcast_to(last, (N, 128))
-        move = pltpu.make_async_copy(vtab, tab, local_sem.at[2])
+        move = pltpu.make_async_copy(vtab, tab, local_sem.at[6])
         move.start()
         return move
 
@@ -150,8 +158,9 @@
         for d in (0, 1):
             for j in range(OWN):
                 gd_copy(m, d, 3, j, gd[m].at[d, 3, j]).wait_recv()
-            o = at(-4 * sign[d])
-            for q in (3, 2, 1, 0):
+        for q in (3, 2, 1, 0):
+            for d in (0, 1):
+                o = at(-4 * sign[d])
                 s = sel(at((q + 1) * sign[d]), o)
                 ss[m][d, q] = pick(gd[m].at[d, 3], s)
                 gs_copy(m, d, 0, q, ss[m].at[d, q]).start()
@@ -296,8 +305,9 @@
         for d in (0, 1):
             for q in (3, 2, 1, 0):
                 rr_copy(r, d, 3, q, rr[r].at[d, 3, q]).wait_recv()
-            o = at(4 * sign[d])
-            for s in range(OWN):
+        for s in range(OWN):
+            for d in (0, 1):
+                o = at(4 * sign[d])
                 acc = masked(sel(me, o) == s, grp[r][(4 * sign[d]) % N].astype(F32))
                 for q in (0, 1, 2):
                     acc = acc + masked(sel(at(-(q + 1) * sign[d]), o) == s, rr[r][d, 3, q].astype(F32))
@@ -328,20 +338,17 @@
         if hi > lo:
             pl.loop(lo, hi)(f)
 
-    copies = (
-        pltpu.make_async_copy(c_hbm, cv, local_sem.at[0]),
-        pltpu.make_async_copy(x_hbm, xv, local_sem.at[1]),
-    )
+    copies[2].wait()
     for j in range(OWN):
         gather_first(0, j)
-    for cp in copies:
-        cp.start()
+    copies[0].wait()
+    copies[1].wait()
     move = build_tables()
     loop(0, 4, lambda i: gather_dense(0, i))
     for r in (0, 1):
         tot[r][2 * half] = jnp.zeros(tot[r].shape[1:], F32)
     move.wait()
-    for cp in copies:
+    for cp in copies[3:]:
         cp.wait()
     loop(4, 12, lambda i: gather_dense(0, i))
     gather_select(0)
@@ -370,12 +377,14 @@
             outer_part(0, mine, 0)
             outer_part(0, mine, 1)
             core2(0, theirs).wait_recv()
+            outer_part(0, theirs, 0)
+        elif h == 1:
+            outer_part(0, theirs, 1)
+            groups(0)
         else:
-            outer_part(0, theirs, h - 1)
+            ret_own(0)
 
     gather_tail(1, fill)
-    groups(0)
-    ret_own(0)
     build(1)
     project_part(1, theirs, 0)
     project_part(1, theirs, 1)
@@ -387,18 +396,17 @@
     reduce_start(1)
     ret_raw(0, 2)
     ret_combine(0)
-    loop(0, 3, lambda i: ret_dense(0, i))
+    loop(0, 4, lambda i: ret_dense(0, i))
     reduce_mid(1)
-    loop(3, 8, lambda i: ret_dense(0, i))
+    loop(4, 9, lambda i: ret_dense(0, i))
     reduce_end(1)
     outer_part(1, mine, 0)
     outer_part(1, mine, 1)
-    loop(8, 10, lambda i: ret_dense(0, i))
+    loop(9, 11, lambda i: ret_dense(0, i))
     core2(1, theirs).wait_recv()
     outer_part(1, theirs, 0)
-    loop(10, 11, lambda i: ret_dense(0, i))
+    ret_dense(0, 11)
     outer_part(1, theirs, 1)
-    loop(11, 12, lambda i: ret_dense(0, i))
     groups(1)
     ret_own(1)
     for h in range(3):
@@ -439,7 +447,8 @@
     dma = lambda *shape: pltpu.SemaphoreType.DMA(shape)
     vm = pl.BlockSpec(memory_space=pltpu.VMEM)
     scratch = [
-        bf(segs, rows, feat), bf(segs, rows, feat),
+        bf(segs, rows, feat), bf(segs, rows, feat), bf(OWN, *a_unit), bf(OWN, *b_unit),
+        pltpu.SMEM(adapter_slot.shape, jnp.int32), pltpu.VMEM(seg_adapter.shape, jnp.int32),
         bf(2, 4, 4, *a_unit), bf(2, 4, 4, *b_unit),
         bf(2, 4, 4, *a_unit), bf(2, 4, 4, *b_unit),
         bf(2, 4, *a_unit), bf(2, 4, *b_unit),
@@ -452,7 +461,7 @@
         bf(2, 4, 4, *a_unit), bf(2, 4, 4, *b_unit),
         bf(2, 4, 4, *a_unit), bf(2, 4, 4, *b_unit),
         pltpu.VMEM((64, 128), jnp.int32), pltpu.SMEM((64, 128), jnp.int32),
-        dma(3),
+        dma(7),
         dma(2, 2), dma(2, 2, 4, 4), dma(2, 2), dma(2, 2, 10),
         dma(2, 2), dma(2, 2, 10), dma(2, 2), dma(2, 2, 4, 4),
     ] + [dma(2)] * 8
@@ -463,12 +472,8 @@
             jax.ShapeDtypeStruct((OWN,) + b_unit, BF16),
         ),
         in_specs=[
-            pl.BlockSpec(memory_space=pltpu.SMEM),
-            vm,
             pl.BlockSpec(memory_space=pl.ANY),
-            pl.BlockSpec(memory_space=pl.ANY),
-            vm, vm,
-        ],
+        ] * 6,
         out_specs=(vm, vm),
         scratch_shapes=scratch,
         compiler_params=pltpu.CompilerParams(

time: 168 us -> 165 us (0.982)
  Pallas kernels: 167 us -> 163 us
    pallas_call x1, Pallas kernels: 165 us -> 162 us  [body(): pl.pallas_call(functools.partial(kernel, segs, chips, per), out_shape=(ja...]
where the time goes in v4:
time: 165 us; the launch traced here: 164 us
  Pallas kernels  163 us (99%)
    pallas_call x1, Pallas kernels, body(): pl.pallas_call(functools.partial(kernel, segs, chips, per), out_shape=(ja...  162 us

profile of v4, /device:TPU:1, one launch (start us, length us, event | category | flops | bytes accessed | tf_op | source)
XLA Modules:
  0.0 164.0 jit_solution(13890076895870751571)
XLA Ops:
  0.6 161.6 %adapter_backward.1 = (bf16[4,2,128,128]{3,2,1,0:T(8,128)(2,1)}, bf16[4,2,64,256]{3,2,1,0:T(8,128)(2,1)}) custom-call(s32[64]{0:T(128)} %slot_hbm.1, s32[16,30]{1,0:T(8,128)} %seg_hbm.1, bf16[30,128,256]{2,1,0:T(8,128)(2,1)} %bitcast.6, bf16[30,128,256]{2,1,0:T(8,128)(2,1)} %bitcast.7, bf16[4,2,128,128]{3,2,1,0:T(8,128)(2,1)} %bitcast.8, ...), custom_call_target="tpu_custom_call" | custom-call | tf_op jit(solution)/shard_map/adapter_backward/pallas_call | solution.py:468
  162.2 1.8 %finish.1 = (bf16[4,2,128,128]{3,2,1,0:T(8,128)(2,1)}, bf16[4,2,64,256]{3,2,1,0:T(8,128)(2,1)}) custom-call(bf16[4,2,128,128]{3,2,1,0:T(8,128)(2,1)} %get-tuple-element.6.a_ref, bf16[4,2,64,256]{3,2,1,0:T(8,128)(2,1)} %get-tuple-element.7.b_ref), custom_call_target="tpu_custom_call" | custom-call | tf_op jit(solution)/shard_map/finish/pallas_call | solution.py:491

commit v5 on v4

--- a/solution.py
+++ b/solution.py
@@ -26,7 +26,7 @@
     ta, tb, ga, gb,
     rra, rrb, rda, rdb, sda, sdb,
     vtab, tab,
-    local_sem, gd_s, gd_r, gs_s, gs_r, rr_s, rr_r, rd_s, rd_r,
+    local_sem, gd_s, gd_r, gs_s, gs_r, rr_s, rd_s,
     c1_s, c1_r, rs_s, rs_r, ag_s, ag_r, c2_s, c2_r,
 ):
     me = lax.axis_index("grp")
@@ -64,6 +64,7 @@
     fac, gd, gs, ss, w, tok = (fb, fa), (gdb, gda), (gsb, gsa), (ssb, ssa), (wb, wa), (cv, xv)
     tot, grp, rr, rd, sd, out = (ta, tb), (ga, gb), (rra, rrb), (rda, rdb), (sda, sdb), (oa, ob)
     sign = (1, -1)
+    rd_r, rr_r = gd_r, gs_r
 
     def at(offset):
         return lax.rem(me + offset + 2 * N, N)
@@ -430,9 +431,17 @@
                 rcopy(span, span, sem.at[m, d], sem.at[m, d], nbr[d]).wait_send()
 
 
-def finish(a_ref, b_ref, oa_ref, ob_ref):
-    oa_ref[...] = a_ref[...]
-    ob_ref[...] = b_ref[...]
+def finish(a_ref, b_ref, oa_ref, ob_ref, a_buf, b_buf, sems):
+    ways = ((a_ref, a_buf, oa_ref), (b_ref, b_buf, ob_ref))
+    loads = [pltpu.make_async_copy(src, buf, sems.at[i]) for i, (src, buf, _) in enumerate(ways)]
+    stores = [pltpu.make_async_copy(buf, dst, sems.at[2 + i]) for i, (_, buf, dst) in enumerate(ways)]
+    for load in loads:
+        load.start()
+    for load, store in zip(loads, stores):
+        load.wait()
+        store.start()
+    for store in stores:
+        store.wait()
 
 
 def body(chips, inputs, cotangent, factor_a, factor_b, adapter_slot, seg_adapter):
@@ -463,7 +472,7 @@
         pltpu.VMEM((64, 128), jnp.int32), pltpu.SMEM((64, 128), jnp.int32),
         dma(7),
         dma(2, 2), dma(2, 2, 4, 4), dma(2, 2), dma(2, 2, 10),
-        dma(2, 2), dma(2, 2, 10), dma(2, 2), dma(2, 2, 4, 4),
+        dma(2, 2), dma(2, 2),
     ] + [dma(2)] * 8
     grad_a, grad_b = pl.pallas_call(
         functools.partial(kernel, segs, chips, per),
@@ -491,8 +500,9 @@
     grad_a, grad_b = pl.pallas_call(
         finish,
         out_shape=(jax.ShapeDtypeStruct(grad_a.shape, BF16), jax.ShapeDtypeStruct(grad_b.shape, BF16)),
-        in_specs=[vm, vm],
-        out_specs=(vm, vm),
+        in_specs=[pl.BlockSpec(memory_space=pl.ANY)] * 2,
+        out_specs=(pl.BlockSpec(memory_space=pl.ANY),) * 2,
+        scratch_shapes=[bf(OWN, *a_unit), bf(OWN, *b_unit), dma(4)],
         name="finish",
     )(grad_a, grad_b)
     return grad_a.reshape(factor_a.shape), grad_b.reshape(factor_b.shape)

time: 165 us -> 164 us (level)
  no operation moved by 1% of the time
where the time goes in v5:
time: 164 us; the launch traced here: 163 us
  Pallas kernels  162 us (99%)
    pallas_call x1, Pallas kernels, body(): pl.pallas_call(functools.partial(kernel, segs, chips, per), out_shape=(ja...  161 us

profile of v5, /device:TPU:1, one launch (start us, length us, event | category | flops | bytes accessed | tf_op | source)
XLA Modules:
  0.0 163.0 jit_solution(3255133482615941085)
XLA Ops:
  0.6 160.6 %adapter_backward.1 = (bf16[4,2,128,128]{3,2,1,0:T(8,128)(2,1)}, bf16[4,2,64,256]{3,2,1,0:T(8,128)(2,1)}) custom-call(s32[64]{0:T(128)} %slot_hbm.1, s32[16,30]{1,0:T(8,128)} %seg_hbm.1, bf16[30,128,256]{2,1,0:T(8,128)(2,1)} %bitcast.6, bf16[30,128,256]{2,1,0:T(8,128)(2,1)} %bitcast.7, bf16[4,2,128,128]{3,2,1,0:T(8,128)(2,1)} %bitcast.8, ...), custom_call_target="tpu_custom_call" | custom-call | tf_op jit(solution)/shard_map/adapter_backward/pallas_call | solution.py:477
  161.3 1.8 %finish.1 = (bf16[4,2,128,128]{3,2,1,0:T(8,128)(2,1)}, bf16[4,2,64,256]{3,2,1,0:T(8,128)(2,1)}) custom-call(bf16[4,2,128,128]{3,2,1,0:T(8,128)(2,1)} %get-tuple-element.6.a_ref, bf16[4,2,64,256]{3,2,1,0:T(8,128)(2,1)} %get-tuple-element.7.b_ref), custom_call_target="tpu_custom_call" | custom-call | tf_op jit(solution)/shard_map/finish/pallas_call | solution.py:500
